TPU v7x, 32 devices: a whole 2x2x4 slice. The times are simulated.
32 devices in a mesh: dp: 4 (over y, x), expert: 8 (over z, core).
Axes of the slice: x: 2, y: 2, z: 4, core: 2. Of those that a mesh axis runs over, the one named last changes fastest.
Arguments:
- tokens: bfloat16 [4096, 7168], P(('dp', 'expert')), may hold values from -6 to 6
- route_ids: int32 [4096, 8], P(('dp', 'expert')), may hold values from 0 to 255, as said below
- gate_weights: float32 [4096, 8], P(('dp', 'expert')), may hold values from 0.3 to 1.2
- gate_weight: bfloat16 [8, 7168, 1024], P('expert', 'dp'), may hold values from -0.0625 to 0.0625
- up_weight: bfloat16 [8, 7168, 1024], P('expert', 'dp'), may hold values from -0.0625 to 0.0625
- down_weight: bfloat16 [8, 7168, 1024], P('expert', 'dp'), may hold values from -0.1875 to 0.1875
- cotangent: bfloat16 [4096, 7168], P(('dp', 'expert')), may hold values from -3 to 3
Outputs:
- output: bfloat16 [4096, 7168], P(('dp', 'expert'))
- grad_tokens: bfloat16 [4096, 7168], P(('dp', 'expert'))
- grad_gate: bfloat16 [8, 7168, 1024], P('expert', 'dp')
- grad_up: bfloat16 [8, 7168, 1024], P('expert', 'dp')
- grad_down: bfloat16 [8, 7168, 1024], P('expert', 'dp')
Inputs may be any that keep to these rules, and one draw needn't show every extreme that they name: `route_ids`: each token's 8 numbers are different, and at most one of them is below 8. Among the 128 tokens of one device at most 4 name any one number below 8; for each index of dp, one number below 8 is named by exactly 4 tokens of every device with that index.
All inputs are finite; a program needn't handle non-finite values.
Results may differ from a plain program's by a relative error of at most 0.018.
Values may be sent and summed in bfloat16 or wider, within the bound.
No kernel may reach another device: no remote copies, remote signals or barrier semaphores. Data moves between devices by JAX's collectives and lax.ppermute only.
A program may use at most 128 MiB of HBM per device.

v0:
```python
import jax
import jax.numpy as jnp
from jax import lax
from jax.sharding import PartitionSpec as P

CAP = 4


def contract_last(left, right):
    return lax.dot_general(
        left, right, (((1,), (1,)), ((), ())), preferred_element_type=jnp.float32
    )


def contract_first(left, right):
    return lax.dot_general(
        left, right, (((0,), (0,)), ((), ())), preferred_element_type=jnp.float32
    )


def body(tokens, route_ids, gate_weights, gate_weight, up_weight, down_weight, cotangent):
    experts = lax.axis_size("expert")
    gate_mat = gate_weight[0]
    up_mat = up_weight[0]
    down_mat = down_weight[0]
    slice_width = gate_mat.shape[0]
    hidden_units = gate_mat.shape[1]
    labels = jnp.arange(experts, dtype=jnp.int32)
    matches = route_ids[:, :, None] == labels
    chosen = jnp.any(matches, axis=1).astype(jnp.int32)
    gate_of = jnp.sum(jnp.where(matches, gate_weights[:, :, None], 0.0), axis=1)
    ranks = jnp.cumsum(chosen, axis=0) - chosen
    placed = (chosen[:, :, None] == 1) & (ranks[:, :, None] == jnp.arange(CAP, dtype=jnp.int32))
    placer = placed.astype(jnp.bfloat16)
    slot_gate = jnp.sum(jnp.where(placed, gate_of[:, :, None], 0.0), axis=0)
    send_rows = jnp.einsum(
        "tjc,td->jcd", placer, tokens, preferred_element_type=jnp.float32
    ).astype(jnp.bfloat16)
    picked = jnp.einsum("tjc,td->jcd", placer, cotangent, preferred_element_type=jnp.float32)
    send_grads = (slot_gate[:, :, None] * picked).astype(jnp.bfloat16)
    recv_rows, recv_grads = (
        lax.all_to_all(
            lax.all_to_all(send_rows, "dp", split_axis=2, concat_axis=1, tiled=True),
            "expert",
            split_axis=0,
            concat_axis=0,
            tiled=True,
        ),
        lax.all_to_all(
            lax.all_to_all(send_grads, "dp", split_axis=2, concat_axis=1, tiled=True),
            "expert",
            split_axis=0,
            concat_axis=0,
            tiled=True,
        ),
    )
    layout = recv_rows.shape
    row_count = layout[0] * layout[1]
    flat_rows = recv_rows.reshape(row_count, slice_width)
    flat_grads = recv_grads.reshape(row_count, slice_width)
    row_block = flat_rows
    grad_block = flat_grads
    mine = lax.psum_scatter(
        jnp.concatenate(
            [
                jnp.dot(row_block, gate_mat, preferred_element_type=jnp.float32),
                jnp.dot(row_block, up_mat, preferred_element_type=jnp.float32),
                jnp.dot(grad_block, down_mat, preferred_element_type=jnp.float32),
            ],
            axis=1,
        ).astype(jnp.bfloat16),
        "dp",
        scatter_dimension=0,
        tiled=True,
    ).astype(jnp.float32)
    pre_gate = mine[:, :hidden_units]
    pre_up = mine[:, hidden_units : 2 * hidden_units]
    hidden_grad = mine[:, 2 * hidden_units :]
    squash = jax.nn.sigmoid(pre_gate)
    silu_gate = pre_gate * squash
    hidden = (silu_gate * pre_up).astype(jnp.bfloat16)
    gate_grad = (hidden_grad * pre_up * squash * (1.0 + pre_gate * (1.0 - squash))).astype(
        jnp.bfloat16
    )
    up_grad = (hidden_grad * silu_gate).astype(jnp.bfloat16)
    hidden, gate_grad, up_grad = (hidden, gate_grad, up_grad)
    hidden_part = lax.all_gather(hidden, "dp", axis=0, tiled=True)
    gate_part = lax.all_gather(gate_grad, "dp", axis=0, tiled=True)
    up_part = lax.all_gather(up_grad, "dp", axis=0, tiled=True)
    row_block = flat_rows
    grad_block = flat_grads
    out_part = contract_last(hidden_part, down_mat).astype(jnp.bfloat16)
    input_part = (contract_last(gate_part, gate_mat) + contract_last(up_part, up_mat)).astype(
        jnp.bfloat16
    )
    out_rows = out_part
    input_rows = input_part
    gate_total = contract_first(row_block, gate_part)
    up_total = contract_first(row_block, up_part)
    down_total = contract_first(grad_block, hidden_part)
    carry = (out_rows, input_rows, gate_total, up_total, down_total)
    out_rows, input_rows, gate_total, up_total, down_total = carry
    got_out, got_input = (
        lax.all_to_all(
            lax.all_to_all(out_rows.reshape(layout), "dp", split_axis=1, concat_axis=2, tiled=True),
            "expert",
            split_axis=0,
            concat_axis=0,
            tiled=True,
        ),
        lax.all_to_all(
            lax.all_to_all(
                input_rows.reshape(layout), "dp", split_axis=1, concat_axis=2, tiled=True
            ),
            "expert",
            split_axis=0,
            concat_axis=0,
            tiled=True,
        ),
    )
    weighted = slot_gate[:, :, None] * got_out.astype(jnp.float32)
    output = jnp.einsum(
        "tjc,jcd->td", placed.astype(jnp.float32), weighted, precision=lax.Precision.HIGHEST
    ).astype(jnp.bfloat16)
    grad_tokens = jnp.einsum(
        "tjc,jcd->td", placer, got_input, preferred_element_type=jnp.float32
    ).astype(jnp.bfloat16)
    return (
        output,
        grad_tokens,
        gate_total.astype(jnp.bfloat16)[None],
        up_total.astype(jnp.bfloat16)[None],
        down_total.astype(jnp.bfloat16)[None],
    )


def solution(mesh):
    return jax.shard_map(
        body,
        mesh=mesh,
        in_specs=(
            P(("dp", "expert"), None),
            P(("dp", "expert"), None),
            P(("dp", "expert"), None),
            P("expert", "dp", None),
            P("expert", "dp", None),
            P("expert", "dp", None),
            P(("dp", "expert"), None),
        ),
        out_specs=(
            P(("dp", "expert"), None),
            P(("dp", "expert"), None),
            P("expert", "dp", None),
            P("expert", "dp", None),
            P("expert", "dp", None),
        ),
        check_vma=False,
    )
```

profile of v0, /device:TPU:0, one launch (start us, length us, event | category | flops | bytes accessed | tf_op | source)
XLA Modules:
  0.0 243.5 jit_solution(8787925912496322918)
XLA Ops:
  7.2 0.8 fusion.44
  8.7 0.4 convolution_convert_fusion
  9.1 7.2 %copy.72 = bf16[8,4,7168]{0,1,2:T(4,128)(2,1)} copy(bf16[8,4,7168]{2,0,1:T(8,128)(2,1)S(1)} %convolution_convert_fusion) | data formatting | bytes 917504 | tf_op jit(solution)/shard_map/convert_element_type | solution.py:38
  16.3 10.2 %reshape.53 = bf16[4,2,28672]{2,1,0:T(2,128)(2,1)} reshape(bf16[7168,4,8]{2,1,0:T(4,128)(2,1)} %bitcast.83) | data formatting | bytes 917504
  26.5 5.2 %all-to-all-start = ((bf16[4,2,28672]{2,1,0:T(2,128)(2,1)}), bf16[4,2,28672]{2,1,0:T(2,128)(2,1)S(1)}, u32[]{:S(2)}, u32[]{:S(2)}) async-start(bf16[4,2,28672]{2,1,0:T(2,128)(2,1)} %reshape.53), calls=%async_computation | async-start | bytes 917504 | tf_op jit(solution)/shard_map/all_to_all | solution.py:43
  31.8 0.4 fusion.2
  32.2 7.2 %copy.76 = bf16[8,4,7168]{0,1,2:T(4,128)(2,1)} copy(bf16[8,4,7168]{2,0,1:T(8,128)(2,1)S(1)} %fusion.2) | data formatting | bytes 917504 | tf_op jit(solution)/shard_map/convert_element_type | solution.py:40
  39.4 10.1 %reshape.51 = bf16[4,2,28672]{2,1,0:T(2,128)(2,1)} reshape(bf16[7168,4,8]{2,1,0:T(4,128)(2,1)} %bitcast.84) | data formatting | bytes 917504
  49.5 4.2 %all-to-all-start.2 = ((bf16[4,2,28672]{2,1,0:T(2,128)(2,1)}), bf16[4,2,28672]{2,1,0:T(2,128)(2,1)S(1)}, u32[]{:S(2)}, u32[]{:S(2)}) async-start(bf16[4,2,28672]{2,1,0:T(2,128)(2,1)} %reshape.51), calls=%async_computation.2 | async-start | bytes 917504 | tf_op jit(solution)/shard_map/all_to_all | solution.py:50
  53.6 9.8 %reshape.54 = bf16[7168,4,8]{2,1,0:T(4,128)(2,1)} reshape(bf16[4,2,28672]{2,1,0:T(2,128)(2,1)S(1)} %all-to-all-done) | data formatting | bytes 917504
  63.4 8.7 %copy.74 = bf16[8,4,4,1792]{3,0,2,1:T(8,128)(2,1)S(1)} copy(bf16[8,4,4,1792]{0,2,3,1:T(4,128)(2,1)} %bitcast.85) | data formatting | bytes 917504 | tf_op jit(solution)/shard_map/all_to_all | solution.py:43
  72.1 0.8 copy.75
  73.0 4.9 %all-to-all-start.1 = ((bf16[8,16,1792]{2,1,0:T(8,128)(2,1)}), bf16[8,16,1792]{2,1,0:T(8,128)(2,1)S(1)}, u32[]{:S(2)}, u32[]{:S(2)}) async-start(bf16[8,16,1792]{2,1,0:T(8,128)(2,1)} %copy.75), calls=%async_computation.1 | async-start | bytes 917504 | tf_op jit(solution)/shard_map/all_to_all | solution.py:42
  77.9 9.8 %reshape.52 = bf16[7168,4,8]{2,1,0:T(4,128)(2,1)} reshape(bf16[4,2,28672]{2,1,0:T(2,128)(2,1)S(1)} %all-to-all-done.2) | data formatting | bytes 917504
  87.7 8.7 %copy.78 = bf16[8,4,4,1792]{3,0,2,1:T(8,128)(2,1)S(1)} copy(bf16[8,4,4,1792]{0,2,3,1:T(4,128)(2,1)} %bitcast.86) | data formatting | bytes 917504 | tf_op jit(solution)/shard_map/all_to_all | solution.py:50
  96.4 0.8 copy.79
  97.2 5.1 %all-to-all-start.3 = ((bf16[8,16,1792]{2,1,0:T(8,128)(2,1)}), bf16[8,16,1792]{2,1,0:T(8,128)(2,1)S(1)}, u32[]{:S(2)}, u32[]{:S(2)}) async-start(bf16[8,16,1792]{2,1,0:T(8,128)(2,1)} %copy.79), calls=%async_computation.3 | async-start | bytes 917504 | tf_op jit(solution)/shard_map/all_to_all | solution.py:49
  102.3 2.8 %fusion.32 = bf16[128,1024]{1,0:T(8,128)(2,1)S(1)} fusion(bf16[128,1792]{1,0:T(8,128)(2,1)S(1)} %bitcast.87, bf16[1,1792,1024]{2,1,0:T(8,128)(2,1)} %param.11), kind=kOutput, calls=%fused_computation.31 | convolution fusion | flops 469893120 | bytes 4390912 | tf_op jit(solution)/shard_map/dot_general | solution.py:67
  105.5 0.6 fusion.29
  106.1 10.1 %all-to-all-done.3 = bf16[8,16,1792]{2,1,0:T(8,128)(2,1)S(1)} async-done(((bf16[8,16,1792]{2,1,0:T(8,128)(2,1)}), bf16[8,16,1792]{2,1,0:T(8,128)(2,1)S(1)}, u32[]{:S(2)}, u32[]{:S(2)}) %all-to-all-start.3) | async-done | bytes 458784 | tf_op jit(solution)/shard_map/all_to_all | solution.py:49
  116.2 2.7 %fusion.35 = bf16[128,1024]{1,0:T(8,128)(2,1)S(1)} fusion(bf16[128,1792]{1,0:T(8,128)(2,1)S(1)} %bitcast.91, bf16[1,1792,1024]{2,1,0:T(8,128)(2,1)} %param.12), kind=kOutput, calls=%fused_computation.32 | convolution fusion | flops 469893120 | bytes 4390912 | tf_op jit(solution)/shard_map/dot_general | solution.py:68
  118.9 0.9 pad_maximum_fusion
  119.9 25.7 %reduce-scatter.2.cloned.1.call-done = bf16[32,3072]{1,0:T(8,128)(2,1)} async-done(((bf16[128,3072]{1,0:T(8,128)(2,1)}), bf16[32,3072]{1,0:T(8,128)(2,1)}) %reduce-scatter.2.cloned.1.call-update) | async-done | bytes 196624 | tf_op jit(solution)/shard_map/reduce_scatter | solution.py:63
  145.6 1.0 convert_element_type.62
  146.6 9.1 %all_gather.10 = bf16[128,1024]{1,0:T(8,128)(2,1)S(1)} all-gather(bf16[32,1024]{1,0:T(8,128)(2,1)S(1)} %get-tuple-element.5), channel_id=1, replica_groups=mesh['dp'=4,'expert'=8] {'dp'}, dimensions={0}, use_global_device_ids=true | all-gather | bytes 327680 | tf_op jit(solution)/shard_map/all_gather | solution.py:88
  155.7 8.4 %all_gather.9 = bf16[128,1024]{1,0:T(8,128)(2,1)S(1)} all-gather(bf16[32,1024]{1,0:T(8,128)(2,1)S(1)} %get-tuple-element.6), channel_id=1, replica_groups=mesh['dp'=4,'expert'=8] {'dp'}, dimensions={0}, use_global_device_ids=true | all-gather | bytes 327680 | tf_op jit(solution)/shard_map/all_gather | solution.py:87
  164.1 9.0 %all_gather.11 = bf16[128,1024]{1,0:T(8,128)(2,1)S(1)} all-gather(bf16[32,1024]{1,0:T(8,128)(2,1)S(1)} %get-tuple-element.7), channel_id=1, replica_groups=mesh['dp'=4,'expert'=8] {'dp'}, dimensions={0}, use_global_device_ids=true | all-gather | bytes 327680 | tf_op jit(solution)/shard_map/all_gather | solution.py:89
  173.2 3.4 %fusion.21 = bf16[128,1792]{1,0:T(8,128)(2,1)S(1)} fusion(bf16[128,1024]{1,0:T(8,128)(2,1)S(1)} %all_gather.9, bf16[1,1792,1024]{2,1,0:T(8,128)(2,1)} %param.12), kind=kOutput, calls=%fused_computation.26 | convolution fusion | flops 469991424 | bytes 4390912 | tf_op jit(solution)/shard_map/dot_general | solution.py:10
  176.5 0.9 copy.80
  177.4 3.5 %all-to-all-start.4 = ((bf16[8,16,1792]{2,0,1:T(8,128)(2,1)}), bf16[8,16,1792]{2,0,1:T(8,128)(2,1)S(1)}, u32[]{:S(2)}, u32[]{:S(2)}) async-start(bf16[8,16,1792]{2,0,1:T(8,128)(2,1)} %copy.80), calls=%async_computation.5 | async-start | bytes 917504 | tf_op jit(solution)/shard_map/all_to_all | solution.py:105
  180.9 3.5 %fusion.7 = f32[128,1792]{1,0:T(8,128)S(1)} fusion(bf16[128,1024]{1,0:T(8,128)(2,1)S(1)} %all_gather.11, bf16[1,1792,1024]{2,1,0:T(8,128)(2,1)} %param.11), kind=kOutput, calls=%fused_computation.14 | convolution fusion | flops 469762048 | bytes 4849664 | tf_op jit(solution)/shard_map/dot_general | solution.py:10
  184.5 1.4 fusion.24
  185.8 0.9 copy.84
  186.7 0.6 all-to-all-done.4
  187.4 3.5 %all-to-all-start.6 = ((bf16[8,16,1792]{2,0,1:T(8,128)(2,1)}), bf16[8,16,1792]{2,0,1:T(8,128)(2,1)S(1)}, u32[]{:S(2)}, u32[]{:S(2)}) async-start(bf16[8,16,1792]{2,0,1:T(8,128)(2,1)} %copy.84), calls=%async_computation.7 | async-start | bytes 917504 | tf_op jit(solution)/shard_map/all_to_all | solution.py:112
  190.9 0.4 copy.91
  191.2 0.9 reshape.50
  192.2 4.9 %all-to-all-done.6 = bf16[8,16,1792]{2,0,1:T(8,128)(2,1)S(1)} async-done(((bf16[8,16,1792]{2,0,1:T(8,128)(2,1)}), bf16[8,16,1792]{2,0,1:T(8,128)(2,1)S(1)}, u32[]{:S(2)}, u32[]{:S(2)}) %all-to-all-start.6) | async-done | bytes 458784 | tf_op jit(solution)/shard_map/all_to_all | solution.py:112
  197.1 4.6 %all-to-all-start.5 = ((bf16[8,4,7168]{2,1,0:T(4,128)(2,1)}), bf16[8,4,7168]{2,1,0:T(4,128)(2,1)S(1)}, u32[]{:S(2)}, u32[]{:S(2)}) async-start(bf16[8,4,7168]{2,1,0:T(4,128)(2,1)} %reshape.50), calls=%async_computation.6 | async-start | bytes 917504 | tf_op jit(solution)/shard_map/all_to_all | solution.py:104
  202.1 0.9 all_to_all.82
  203.0 12.6 %all-to-all-done.5 = bf16[8,4,7168]{2,1,0:T(4,128)(2,1)S(1)} async-done(((bf16[8,4,7168]{2,1,0:T(4,128)(2,1)}), bf16[8,4,7168]{2,1,0:T(4,128)(2,1)S(1)}, u32[]{:S(2)}, u32[]{:S(2)}) %all-to-all-start.5) | async-done | bytes 458784 | tf_op jit(solution)/shard_map/all_to_all | solution.py:104
  215.7 4.1 %all-to-all-start.7 = ((bf16[8,4,7168]{2,1,0:T(4,128)(2,1)}), bf16[8,4,7168]{2,1,0:T(4,128)(2,1)}, u32[]{:S(2)}, u32[]{:S(2)}) async-start(bf16[8,4,7168]{2,1,0:T(4,128)(2,1)} %all_to_all.82), calls=%async_computation.8 | async-start | bytes 917504 | tf_op jit(solution)/shard_map/all_to_all | solution.py:111
  219.8 3.0 %fusion.17 = bf16[1,1792,1024]{2,1,0:T(8,128)(2,1)} fusion(bf16[128,1792]{1,0:T(8,128)(2,1)S(1)} %bitcast.92, bf16[128,1024]{1,0:T(8,128)(2,1)S(1)} %all_gather.9), kind=kOutput, calls=%fused_computation.24 | convolution fusion | flops 471597056 | bytes 4390912 | tf_op jit(solution)/shard_map/dot_general | solution.py:16
  222.8 3.0 %fusion.15 = bf16[1,1792,1024]{2,1,0:T(8,128)(2,1)} fusion(bf16[128,1792]{1,0:T(8,128)(2,1)S(1)} %bitcast.89, bf16[128,1024]{1,0:T(8,128)(2,1)S(1)} %all_gather.10), kind=kOutput, calls=%fused_computation.22 | convolution fusion | flops 471597056 | bytes 4390912 | tf_op jit(solution)/shard_map/dot_general | solution.py:16
  225.7 3.0 %fusion.16 = bf16[1,1792,1024]{2,1,0:T(8,128)(2,1)} fusion(bf16[128,1792]{1,0:T(8,128)(2,1)S(1)} %bitcast.90, bf16[128,1024]{1,0:T(8,128)(2,1)S(1)} %all_gather.11), kind=kOutput, calls=%fused_computation.23 | convolution fusion | flops 471597056 | bytes 4390912 | tf_op jit(solution)/shard_map/dot_general | solution.py:16
  228.7 2.9 %fusion = bf16[128,7168]{1,0:T(8,128)(2,1)} fusion(bf16[8,4,7168]{2,1,0:T(4,128)(2,1)S(1)} %all-to-all-done.5, f32[8,4]{0,1:T(4,128)S(1)} %select_reduce_fusion.1, s32[128,8]{0,1:T(8,128)S(1)} %copy.71, pred[128,8]{0,1:T(8,128)(4,1)S(1)} %copy.70), kind=kOutput, calls=%fused_computation.2 | convolution fusion | flops 353705984 | bytes 2299008 | tf_op jit(solution)/shard_map/tjc,jcd->td/dot_general | solution.py:122
  231.7 2.1 all-to-all-done.7
  233.7 2.9 %fusion.1 = bf16[128,7168]{1,0:T(8,128)(2,1)} fusion(bf16[8,4,7168]{2,1,0:T(4,128)(2,1)} %all-to-all-done.7, s32[128,8]{0,1:T(8,128)S(1)} %copy.71, pred[128,8]{0,1:T(8,128)(4,1)S(1)} %copy.70), kind=kOutput, calls=%fused_computation.3 | convolution fusion | flops 59645952 | bytes 2298880 | tf_op jit(solution)/shard_map/tjc,jcd->td/dot_general | solution.py:125
  (29 shorter events, 1.6 us)
Async XLA Ops:
  7.2 1.5 copy-start
  16.3 15.4 %copy-start.5 = (s32[128,8]{0,1:T(8,128)S(1)}, s32[128,8]{0,1:T(8,128)}, u32[]{:S(2)}) copy-start(s32[128,8]{0,1:T(8,128)} %param.8) | copy-start | bytes 12292
  16.3 15.4 %copy-start.6 = (f32[128,8]{0,1:T(8,128)S(1)}, f32[128,8]{0,1:T(8,128)}, u32[]{:S(2)}) copy-start(f32[128,8]{0,1:T(8,128)} %param.9) | copy-start | bytes 12292
  16.3 15.5 %copy-start.4 = (bf16[128,7168]{1,0:T(8,128)(2,1)S(1)}, bf16[128,7168]{1,0:T(8,128)(2,1)}, u32[]{:S(2)}) copy-start(bf16[128,7168]{1,0:T(8,128)(2,1)} %param.13) | copy-start | bytes 5505028
  26.5 23.0 %all-to-all-start = ((bf16[4,2,28672]{2,1,0:T(2,128)(2,1)}), bf16[4,2,28672]{2,1,0:T(2,128)(2,1)S(1)}, u32[]{:S(2)}, u32[]{:S(2)}) async-start(bf16[4,2,28672]{2,1,0:T(2,128)(2,1)} %reshape.53), calls=%async_computation | async-start | bytes 917504 | tf_op jit(solution)/shard_map/all_to_all | solution.py:43
  49.5 23.5 %all-to-all-start.2 = ((bf16[4,2,28672]{2,1,0:T(2,128)(2,1)}), bf16[4,2,28672]{2,1,0:T(2,128)(2,1)S(1)}, u32[]{:S(2)}, u32[]{:S(2)}) async-start(bf16[4,2,28672]{2,1,0:T(2,128)(2,1)} %reshape.51), calls=%async_computation.2 | async-start | bytes 917504 | tf_op jit(solution)/shard_map/all_to_all | solution.py:50
  73.0 24.2 %all-to-all-start.1 = ((bf16[8,16,1792]{2,1,0:T(8,128)(2,1)}), bf16[8,16,1792]{2,1,0:T(8,128)(2,1)S(1)}, u32[]{:S(2)}, u32[]{:S(2)}) async-start(bf16[8,16,1792]{2,1,0:T(8,128)(2,1)} %copy.75), calls=%async_computation.1 | async-start | bytes 917504 | tf_op jit(solution)/shard_map/all_to_all | solution.py:42
  97.2 19.0 %all-to-all-start.3 = ((bf16[8,16,1792]{2,1,0:T(8,128)(2,1)}), bf16[8,16,1792]{2,1,0:T(8,128)(2,1)S(1)}, u32[]{:S(2)}, u32[]{:S(2)}) async-start(bf16[8,16,1792]{2,1,0:T(8,128)(2,1)} %copy.79), calls=%async_computation.3 | async-start | bytes 917504 | tf_op jit(solution)/shard_map/all_to_all | solution.py:49
  102.3 43.3 %reduce-scatter.2.cloned.1.call-start = ((), (), s32[]{:S(2)}) async-start(), calls=%async_computation.9 | async-start | bytes 983040 | tf_op jit(solution)/shard_map/reduce_scatter | solution.py:63
  102.3 3.1 %copy-start.2 = (bf16[1,1792,1024]{2,1,0:T(8,128)(2,1)S(1)}, bf16[1,1792,1024]{2,1,0:T(8,128)(2,1)}, u32[]{:S(2)}) copy-start(bf16[1,1792,1024]{2,1,0:T(8,128)(2,1)} %param.10) | copy-start | bytes 11010052
  177.4 9.9 %all-to-all-start.4 = ((bf16[8,16,1792]{2,0,1:T(8,128)(2,1)}), bf16[8,16,1792]{2,0,1:T(8,128)(2,1)S(1)}, u32[]{:S(2)}, u32[]{:S(2)}) async-start(bf16[8,16,1792]{2,0,1:T(8,128)(2,1)} %copy.80), calls=%async_computation.5 | async-start | bytes 917504 | tf_op jit(solution)/shard_map/all_to_all | solution.py:105
  180.9 3.5 %copy-start.3 = (bf16[1,1792,1024]{2,1,0:T(8,128)(2,1)S(1)}, bf16[1,1792,1024]{2,1,0:T(8,128)(2,1)}, u32[]{:S(2)}) copy-start(bf16[1,1792,1024]{2,1,0:T(8,128)(2,1)} %param.10) | copy-start | bytes 11010052
  187.4 9.8 %all-to-all-start.6 = ((bf16[8,16,1792]{2,0,1:T(8,128)(2,1)}), bf16[8,16,1792]{2,0,1:T(8,128)(2,1)S(1)}, u32[]{:S(2)}, u32[]{:S(2)}) async-start(bf16[8,16,1792]{2,0,1:T(8,128)(2,1)} %copy.84), calls=%async_computation.7 | async-start | bytes 917504 | tf_op jit(solution)/shard_map/all_to_all | solution.py:112
  197.1 18.5 %all-to-all-start.5 = ((bf16[8,4,7168]{2,1,0:T(4,128)(2,1)}), bf16[8,4,7168]{2,1,0:T(4,128)(2,1)S(1)}, u32[]{:S(2)}, u32[]{:S(2)}) async-start(bf16[8,4,7168]{2,1,0:T(4,128)(2,1)} %reshape.50), calls=%async_computation.6 | async-start | bytes 917504 | tf_op jit(solution)/shard_map/all_to_all | solution.py:104
  215.7 18.1 %all-to-all-start.7 = ((bf16[8,4,7168]{2,1,0:T(4,128)(2,1)}), bf16[8,4,7168]{2,1,0:T(4,128)(2,1)}, u32[]{:S(2)}, u32[]{:S(2)}) async-start(bf16[8,4,7168]{2,1,0:T(4,128)(2,1)} %all_to_all.82), calls=%async_computation.8 | async-start | bytes 917504 | tf_op jit(solution)/shard_map/all_to_all | solution.py:111
  222.8 13.9 %copy-start.1 = (bf16[128,7168]{1,0:T(8,128)(2,1)S(1)}, bf16[128,7168]{1,0:T(8,128)(2,1)}, u32[]{:S(2)}) copy-start(bf16[128,7168]{1,0:T(8,128)(2,1)} %param.7) | copy-start | bytes 5505028
Sparse Core Ops, SparseCore 0:
  120.0 25.5 reduce-scatter.1
where the time goes:
time: 245 us; the launch traced here: 243 us
  local copies, waits for them, and re-layouts  78.5 us (32%)
  waiting for transfers between devices  56.1 us (23%)
  starting transfers between devices  35.1 us (14%)
  matrix products  29.9 us (12%)
  blocking collectives  26.5 us (11%)
  between operations  14.2 us (6%)
  other arithmetic  3.11 us (1%)
    unnamed x18, local copies, waits for them, and re-layouts  40.4 us
    reduce_scatter x1, waiting for transfers between devices, body(): lax.psum_scatter(jnp.concatenate([jnp.dot(row_block, gate_mat, preferred_...  25.7 us
    all_to_all x1, waiting for transfers between devices, body(): lax.all_to_all(lax.all_to_all(out_rows.reshape(layout), 'dp', split_axis=...  12.6 us
    all_to_all x1, waiting for transfers between devices, body(): lax.all_to_all(lax.all_to_all(send_grads, 'dp', split_axis=2, concat_axis...  10.1 us
    all_to_all x2, local copies, waits for them, and re-layouts, body(): lax.all_to_all(send_rows, 'dp', split_axis=2, concat_axis=1, tiled=True)  9.54 us
    all_to_all x2, local copies, waits for them, and re-layouts, body(): lax.all_to_all(send_grads, 'dp', split_axis=2, concat_axis=1, tiled=True)  9.54 us
    all_gather x1, blocking collectives, body(): gate_part = lax.all_gather(gate_grad, 'dp', axis=0, tiled=True)  9.05 us
    all_gather x1, blocking collectives, body(): up_part = lax.all_gather(up_grad, 'dp', axis=0, tiled=True)  9.04 us
  transfers between devices with their start and end apart: 9, of which 6 were waited for; matrix products, arithmetic and copies ran while one was open for 33% of the time, Pallas kernels for 0%

commit v1 on v0

--- a/solution.py
+++ b/solution.py
@@ -4,6 +4,22 @@
 from jax.sharding import PartitionSpec as P
 
 CAP = 4
+
+
+def swapped_with_each(x, axis, split, join):
+    ways, here = (lax.axis_size(axis), lax.axis_index(axis))
+    width = x.shape[split] // ways
+    lengths = list(x.shape)
+    lengths[split] = width
+    height = lengths[join]
+    lengths[join] = height * ways
+    full = jnp.zeros(lengths, x.dtype)
+    for mask in range(ways):
+        part = lax.dynamic_slice_in_dim(x, (here ^ mask) * width, width, axis=split)
+        if mask:
+            part = lax.ppermute(part, axis, [(d, d ^ mask) for d in range(ways)])
+        full = lax.dynamic_update_slice_in_dim(full, part, (here ^ mask) * height, axis=join)
+    return full
 
 
 def contract_last(left, right):
@@ -47,7 +63,7 @@
             tiled=True,
         ),
         lax.all_to_all(
-            lax.all_to_all(send_grads, "dp", split_axis=2, concat_axis=1, tiled=True),
+            swapped_with_each(send_grads, "dp", 2, 1),
             "expert",
             split_axis=0,
             concat_axis=0,

time: 245 us -> 219 us (0.89)
  local copies, waits for them, and re-layouts: 78.5 us -> 50.8 us
  waiting for transfers between devices: 56.1 us -> 52.4 us
    unnamed x18 -> x8, local copies, waits for them, and re-layouts: 40.4 us -> 20.2 us
    all_to_all x1, waiting for transfers between devices: 0.01 us -> 11.2 us  [body(): lax.all_to_all(lax.all_to_all(send_rows, 'dp', split_axis=2, concat_axis=...]
    all_to_all x1, waiting for transfers between devices: 12.6 us -> 2.06 us  [body(): lax.all_to_all(lax.all_to_all(out_rows.reshape(layout), 'dp', split_axis=...]
    all_to_all x2 -> x1, waiting for transfers between devices: 10.1 us -> 0.01 us  [body(): lax.all_to_all(swapped_with_each(send_grads, 'dp', 2, 1), 'expert', split...]
    all_to_all x2 -> x0, local copies, waits for them, and re-layouts: 9.54 us -> none  [body(): lax.all_to_all(send_grads, 'dp', split_axis=2, concat_axis=1, tiled=True)]
    all_to_all x1, waiting for transfers between devices: 2.05 us -> 9.93 us  [body(): lax.all_to_all(lax.all_to_all(input_rows.reshape(layout), 'dp', split_axi...]
    convert_element_type x1 -> x0, local copies, waits for them, and re-layouts: 7.2 us -> none  [body(): send_grads = (slot_gate[:, :, None] * picked).astype(jnp.bfloat16)]
    all_to_all x1, waiting for transfers between devices: 4.93 us -> 0.01 us  [body(): lax.all_to_all(input_rows.reshape(layout), 'dp', split_axis=1, concat_axi...]
  transfers between devices with their start and end apart: 9 -> 11, of which waited for: 6 -> 6; matrix products, arithmetic and copies ran while one was open for 33% -> 31% of each run, Pallas kernels for 0% -> 0%
where the time goes in v1:
time: 219 us; the launch traced here: 218 us
  waiting for transfers between devices  52.4 us (24%)
  local copies, waits for them, and re-layouts  50.8 us (23%)
  starting transfers between devices  35.9 us (16%)
  matrix products  32.3 us (15%)
  blocking collectives  27.6 us (13%)
  between operations  14.2 us (6%)
  other arithmetic  4.6 us (2%)
    reduce_scatter x1, waiting for transfers between devices, body(): lax.psum_scatter(jnp.concatenate([jnp.dot(row_block, gate_mat, preferred_...  24.3 us
    unnamed x8, local copies, waits for them, and re-layouts  20.2 us
    all_to_all x1, waiting for transfers between devices, body(): lax.all_to_all(lax.all_to_all(send_rows, 'dp', split_axis=2, concat_axis=...  11.2 us
    all_gather x1, blocking collectives, body(): hidden_part = lax.all_gather(hidden, 'dp', axis=0, tiled=True)  10.7 us
    all_to_all x1, waiting for transfers between devices, body(): lax.all_to_all(lax.all_to_all(input_rows.reshape(layout), 'dp', split_axi...  9.93 us
    all_to_all x2, local copies, waits for them, and re-layouts, body(): lax.all_to_all(send_rows, 'dp', split_axis=2, concat_axis=1, tiled=True)  9.54 us
    all_gather x1, blocking collectives, body(): up_part = lax.all_gather(up_grad, 'dp', axis=0, tiled=True)  9.06 us
    dot_general x3, matrix products, contract_first(): lax.dot_general(left, right, (((0,), (0,)), ((), ())), preferred_element_...  8.94 us
  transfers between devices with their start and end apart: 11, of which 6 were waited for; matrix products, arithmetic and copies ran while one was open for 31% of the time, Pallas kernels for 0%

profile of v1, /device:TPU:0, one launch (start us, length us, event | category | flops | bytes accessed | tf_op | source)
XLA Modules:
  0.0 217.8 jit_solution(6660374598911541907)
XLA Ops:
  7.2 0.8 fusion.44
  8.5 0.7 select_reduce_fusion
  9.8 3.0 %collective-permute-start = (bf16[8,4,1792]{2,0,1:T(8,128)(2,1)S(1)}, bf16[8,4,1792]{2,0,1:T(8,128)(2,1)S(1)}, u32[]{:S(2)}, u32[]{:S(2)}) collective-permute-start(bf16[8,4,1792]{2,0,1:T(8,128)(2,1)S(1)} %get-tuple-element.7), channel_id=1, source_target_pairs={{0,8},{8,0},{16,24},{24,16},{1,9},{9,1},{17,25},{25,17},{2,10},{10... | collective-permute-start | bytes 344072 | tf_op jit(solution)/shard_map/ppermute | solution.py:20
  12.8 1.5 collective-permute-start.1
  14.3 1.9 convolution_convert_fusion
  16.2 7.2 %copy.79 = bf16[8,4,7168]{0,1,2:T(4,128)(2,1)} copy(bf16[8,4,7168]{2,0,1:T(8,128)(2,1)S(1)} %convolution_convert_fusion) | data formatting | bytes 917504 | tf_op jit(solution)/shard_map/convert_element_type | solution.py:54
  23.4 10.1 %reshape.51 = bf16[4,2,28672]{2,1,0:T(2,128)(2,1)} reshape(bf16[7168,4,8]{2,1,0:T(4,128)(2,1)} %bitcast.76) | data formatting | bytes 917504
  33.5 4.2 %all-to-all-start = ((bf16[4,2,28672]{2,1,0:T(2,128)(2,1)}), bf16[4,2,28672]{2,1,0:T(2,128)(2,1)S(1)}, u32[]{:S(2)}, u32[]{:S(2)}) async-start(bf16[4,2,28672]{2,1,0:T(2,128)(2,1)} %reshape.51), calls=%async_computation | async-start | bytes 917504 | tf_op jit(solution)/shard_map/all_to_all | solution.py:59
  37.7 0.8 broadcast_in_dim.49
  39.2 0.7 copy_dynamic-update-slice_fusion.2
  39.9 0.7 copy_dynamic-update-slice_fusion.1
  41.2 2.9 %all-to-all-done = bf16[4,2,28672]{2,1,0:T(2,128)(2,1)S(1)} async-done(((bf16[4,2,28672]{2,1,0:T(2,128)(2,1)}), bf16[4,2,28672]{2,1,0:T(2,128)(2,1)S(1)}, u32[]{:S(2)}, u32[]{:S(2)}) %all-to-all-start) | async-done | bytes 458784 | tf_op jit(solution)/shard_map/all_to_all | solution.py:59
  44.1 4.9 %all-to-all-start.2 = ((bf16[8,16,1792]{2,1,0:T(8,128)(2,1)}), bf16[8,16,1792]{2,1,0:T(8,128)(2,1)S(1)}, u32[]{:S(2)}, u32[]{:S(2)}) async-start(bf16[8,16,1792]{2,1,0:T(8,128)(2,1)} %copy_dynamic-update-slice_fusion), calls=%async_computation.2 | async-start | bytes 917504 | tf_op jit(solution)/shard_map/all_to_all | solution.py:65
  49.0 9.8 %reshape.52 = bf16[7168,4,8]{2,1,0:T(4,128)(2,1)} reshape(bf16[4,2,28672]{2,1,0:T(2,128)(2,1)S(1)} %all-to-all-done) | data formatting | bytes 917504
  58.8 8.7 %copy.81 = bf16[8,4,4,1792]{3,0,2,1:T(8,128)(2,1)S(1)} copy(bf16[8,4,4,1792]{0,2,3,1:T(4,128)(2,1)} %bitcast.77) | data formatting | bytes 917504 | tf_op jit(solution)/shard_map/all_to_all | solution.py:59
  67.5 0.8 copy.82
  68.4 5.1 %all-to-all-start.1 = ((bf16[8,16,1792]{2,1,0:T(8,128)(2,1)}), bf16[8,16,1792]{2,1,0:T(8,128)(2,1)S(1)}, u32[]{:S(2)}, u32[]{:S(2)}) async-start(bf16[8,16,1792]{2,1,0:T(8,128)(2,1)} %copy.82), calls=%async_computation.1 | async-start | bytes 917504 | tf_op jit(solution)/shard_map/all_to_all | solution.py:58
  73.5 2.7 %fusion.35 = bf16[128,1024]{1,0:T(8,128)(2,1)S(1)} fusion(bf16[128,1792]{1,0:T(8,128)(2,1)S(1)} %bitcast.82, bf16[1,1792,1024]{2,1,0:T(8,128)(2,1)} %param.12), kind=kOutput, calls=%fused_computation.32 | convolution fusion | flops 469893120 | bytes 4390912 | tf_op jit(solution)/shard_map/dot_general | solution.py:84
  76.2 11.2 %all-to-all-done.1 = bf16[8,16,1792]{2,1,0:T(8,128)(2,1)S(1)} async-done(((bf16[8,16,1792]{2,1,0:T(8,128)(2,1)}), bf16[8,16,1792]{2,1,0:T(8,128)(2,1)S(1)}, u32[]{:S(2)}, u32[]{:S(2)}) %all-to-all-start.1) | async-done | bytes 458784 | tf_op jit(solution)/shard_map/all_to_all | solution.py:58
  87.4 2.8 %fusion.29 = bf16[128,1024]{1,0:T(8,128)(2,1)S(1)} fusion(bf16[128,1792]{1,0:T(8,128)(2,1)S(1)} %bitcast.78, bf16[1,1792,1024]{2,1,0:T(8,128)(2,1)} %param.10), kind=kOutput, calls=%fused_computation.30 | convolution fusion | flops 469893120 | bytes 4390912 | tf_op jit(solution)/shard_map/dot_general | solution.py:82
  91.2 0.9 pad_maximum_fusion
  92.1 24.3 %reduce-scatter.2.cloned.1.call-done = bf16[32,3072]{1,0:T(8,128)(2,1)} async-done(((bf16[128,3072]{1,0:T(8,128)(2,1)}), bf16[32,3072]{1,0:T(8,128)(2,1)}) %reduce-scatter.2.cloned.1.call-update) | async-done | bytes 196624 | tf_op jit(solution)/shard_map/reduce_scatter | solution.py:79
  116.4 1.1 convert_element_type.62
  117.5 0.7 multiply_convert_fusion.1
  118.2 9.1 %all_gather.11 = bf16[128,1024]{1,0:T(8,128)(2,1)S(1)} all-gather(bf16[32,1024]{1,0:T(8,128)(2,1)S(1)} %get-tuple-element.11), channel_id=1, replica_groups=mesh['dp'=4,'expert'=8] {'dp'}, dimensions={0}, use_global_device_ids=true | all-gather | bytes 327680 | tf_op jit(solution)/shard_map/all_gather | solution.py:105
  127.3 7.9 %all_gather.10 = bf16[128,1024]{1,0:T(8,128)(2,1)S(1)} all-gather(bf16[32,1024]{1,0:T(8,128)(2,1)S(1)} %get-tuple-element.9), channel_id=1, replica_groups=mesh['dp'=4,'expert'=8] {'dp'}, dimensions={0}, use_global_device_ids=true | all-gather | bytes 327680 | tf_op jit(solution)/shard_map/all_gather | solution.py:104
  135.2 3.4 %fusion.7 = f32[128,1792]{1,0:T(8,128)S(1)} fusion(bf16[128,1024]{1,0:T(8,128)(2,1)S(1)} %all_gather.11, bf16[1,1792,1024]{2,1,0:T(8,128)(2,1)} %param.11), kind=kOutput, calls=%fused_computation.14 | convolution fusion | flops 469762048 | bytes 4849664 | tf_op jit(solution)/shard_map/dot_general | solution.py:26
  138.6 1.3 fusion.24
  139.9 0.9 copy.91
  140.8 4.1 %all-to-all-start.5 = ((bf16[8,16,1792]{2,0,1:T(8,128)(2,1)}), bf16[8,16,1792]{2,0,1:T(8,128)(2,1)}, u32[]{:S(2)}, u32[]{:S(2)}) async-start(bf16[8,16,1792]{2,0,1:T(8,128)(2,1)} %copy.91), calls=%async_computation.6 | async-start | bytes 917504 | tf_op jit(solution)/shard_map/all_to_all | solution.py:128
  145.0 10.7 %all_gather.9 = bf16[128,1024]{1,0:T(8,128)(2,1)S(1)} all-gather(bf16[32,1024]{1,0:T(8,128)(2,1)} %get-tuple-element.10), channel_id=1, replica_groups=mesh['dp'=4,'expert'=8] {'dp'}, dimensions={0}, use_global_device_ids=true | all-gather | bytes 327680 | tf_op jit(solution)/shard_map/all_gather | solution.py:103
  155.6 3.4 %fusion.21 = bf16[128,1792]{1,0:T(8,128)(2,1)S(1)} fusion(bf16[128,1024]{1,0:T(8,128)(2,1)S(1)} %all_gather.9, bf16[1,1792,1024]{2,1,0:T(8,128)(2,1)} %param.12), kind=kOutput, calls=%fused_computation.26 | convolution fusion | flops 469991424 | bytes 4390912 | tf_op jit(solution)/shard_map/dot_general | solution.py:26
  159.0 0.9 copy.87
  159.9 4.3 %all-to-all-start.3 = ((bf16[8,16,1792]{2,0,1:T(8,128)(2,1)}), bf16[8,16,1792]{2,0,1:T(8,128)(2,1)}, u32[]{:S(2)}, u32[]{:S(2)}) async-start(bf16[8,16,1792]{2,0,1:T(8,128)(2,1)} %copy.87), calls=%async_computation.4 | async-start | bytes 917504 | tf_op jit(solution)/shard_map/all_to_all | solution.py:121
  164.2 2.1 copy.92
  166.4 2.0 all_to_all.65
  168.3 2.0 all-to-all-done.3
  170.3 4.6 %all-to-all-start.6 = ((bf16[8,4,7168]{2,1,0:T(4,128)(2,1)}), bf16[8,4,7168]{2,1,0:T(4,128)(2,1)}, u32[]{:S(2)}, u32[]{:S(2)}) async-start(bf16[8,4,7168]{2,1,0:T(4,128)(2,1)} %all_to_all.65), calls=%async_computation.7 | async-start | bytes 917504 | tf_op jit(solution)/shard_map/all_to_all | solution.py:127
  174.9 2.1 copy.96
  177.1 2.0 reshape.50
  179.0 9.9 %all-to-all-done.6 = bf16[8,4,7168]{2,1,0:T(4,128)(2,1)} async-done(((bf16[8,4,7168]{2,1,0:T(4,128)(2,1)}), bf16[8,4,7168]{2,1,0:T(4,128)(2,1)}, u32[]{:S(2)}, u32[]{:S(2)}) %all-to-all-start.6) | async-done | bytes 458784 | tf_op jit(solution)/shard_map/all_to_all | solution.py:127
  189.0 4.1 %all-to-all-start.4 = ((bf16[8,4,7168]{2,1,0:T(4,128)(2,1)}), bf16[8,4,7168]{2,1,0:T(4,128)(2,1)}, u32[]{:S(2)}, u32[]{:S(2)}) async-start(bf16[8,4,7168]{2,1,0:T(4,128)(2,1)} %reshape.50), calls=%async_computation.5 | async-start | bytes 917504 | tf_op jit(solution)/shard_map/all_to_all | solution.py:120
  193.1 3.0 %fusion.16 = bf16[1,1792,1024]{2,1,0:T(8,128)(2,1)} fusion(bf16[128,1792]{1,0:T(8,128)(2,1)S(1)} %bitcast.80, bf16[128,1024]{1,0:T(8,128)(2,1)S(1)} %all_gather.11), kind=kOutput, calls=%fused_computation.23 | convolution fusion | flops 471597056 | bytes 4390912 | tf_op jit(solution)/shard_map/dot_general | solution.py:32
  196.1 3.0 %fusion.15 = bf16[1,1792,1024]{2,1,0:T(8,128)(2,1)} fusion(bf16[128,1792]{1,0:T(8,128)(2,1)S(1)} %bitcast.81, bf16[128,1024]{1,0:T(8,128)(2,1)S(1)} %all_gather.10), kind=kOutput, calls=%fused_computation.22 | convolution fusion | flops 471597056 | bytes 4390912 | tf_op jit(solution)/shard_map/dot_general | solution.py:32
  199.0 3.0 %fusion.17 = bf16[1,1792,1024]{2,1,0:T(8,128)(2,1)} fusion(bf16[128,1792]{1,0:T(8,128)(2,1)S(1)} %bitcast.83, bf16[128,1024]{1,0:T(8,128)(2,1)S(1)} %all_gather.9), kind=kOutput, calls=%fused_computation.24 | convolution fusion | flops 471597056 | bytes 4390912 | tf_op jit(solution)/shard_map/dot_general | solution.py:32
  202.0 2.9 %fusion.1 = bf16[128,7168]{1,0:T(8,128)(2,1)} fusion(bf16[8,4,7168]{2,1,0:T(4,128)(2,1)} %all-to-all-done.6, s32[128,8]{0,1:T(8,128)S(1)} %copy.78, pred[128,8]{0,1:T(8,128)(4,1)S(1)} %copy.77), kind=kOutput, calls=%fused_computation.3 | convolution fusion | flops 59645952 | bytes 2298880 | tf_op jit(solution)/shard_map/tjc,jcd->td/dot_general | solution.py:141
  205.0 2.1 all-to-all-done.4
  207.0 3.9 %fusion = bf16[128,7168]{1,0:T(8,128)(2,1)} fusion(bf16[8,4,7168]{2,1,0:T(4,128)(2,1)} %all-to-all-done.4, f32[8,4]{0,1:T(4,128)S(1)} %select_reduce_fusion.1, s32[128,8]{0,1:T(8,128)S(1)} %copy.78, pred[128,8]{0,1:T(8,128)(4,1)S(1)} %copy.77), kind=kOutput, calls=%fused_computation.2 | convolution fusion | flops 353705984 | bytes 2299008 | tf_op jit(solution)/shard_map/tjc,jcd->td/dot_general | solution.py:138
  (26 shorter events, 3.4 us)
Async XLA Ops:
  7.2 2.2 copy-start
  9.8 29.4 %collective-permute-start = (bf16[8,4,1792]{2,0,1:T(8,128)(2,1)S(1)}, bf16[8,4,1792]{2,0,1:T(8,128)(2,1)S(1)}, u32[]{:S(2)}, u32[]{:S(2)}) collective-permute-start(bf16[8,4,1792]{2,0,1:T(8,128)(2,1)S(1)} %get-tuple-element.7), channel_id=1, source_target_pairs={{0,8},{8,0},{16,24},{24,16},{1,9},{9,1},{17,25},{25,17},{2,10},{10... | collective-permute-start | bytes 344072 | tf_op jit(solution)/shard_map/ppermute | solution.py:20
  12.8 27.1 %collective-permute-start.1 = (bf16[8,4,1792]{2,0,1:T(8,128)(2,1)S(1)}, bf16[8,4,1792]{2,0,1:T(8,128)(2,1)S(1)}, u32[]{:S(2)}, u32[]{:S(2)}) collective-permute-start(bf16[8,4,1792]{2,0,1:T(8,128)(2,1)S(1)} %get-tuple-element.6), channel_id=1, source_target_pairs={{0,16},{8,24},{16,0},{24,8},{1,17},{9,25},{17,1},{25,9},{2,18},{10... | collective-permute-start | bytes 344072 | tf_op jit(solution)/shard_map/ppermute | solution.py:20
  14.3 26.2 %collective-permute-start.2 = (bf16[8,4,1792]{2,0,1:T(8,128)(2,1)S(1)}, bf16[8,4,1792]{2,0,1:T(8,128)(2,1)S(1)}, u32[]{:S(2)}, u32[]{:S(2)}) collective-permute-start(bf16[8,4,1792]{2,0,1:T(8,128)(2,1)S(1)} %get-tuple-element.5), channel_id=1, source_target_pairs={{0,24},{8,16},{16,8},{24,0},{1,25},{9,17},{17,9},{25,1},{2,26},{10... | collective-permute-start | bytes 344072 | tf_op jit(solution)/shard_map/ppermute | solution.py:20
  33.5 10.6 %all-to-all-start = ((bf16[4,2,28672]{2,1,0:T(2,128)(2,1)}), bf16[4,2,28672]{2,1,0:T(2,128)(2,1)S(1)}, u32[]{:S(2)}, u32[]{:S(2)}) async-start(bf16[4,2,28672]{2,1,0:T(2,128)(2,1)} %reshape.51), calls=%async_computation | async-start | bytes 917504 | tf_op jit(solution)/shard_map/all_to_all | solution.py:59
  44.1 24.3 %all-to-all-start.2 = ((bf16[8,16,1792]{2,1,0:T(8,128)(2,1)}), bf16[8,16,1792]{2,1,0:T(8,128)(2,1)S(1)}, u32[]{:S(2)}, u32[]{:S(2)}) async-start(bf16[8,16,1792]{2,1,0:T(8,128)(2,1)} %copy_dynamic-update-slice_fusion), calls=%async_computation.2 | async-start | bytes 917504 | tf_op jit(solution)/shard_map/all_to_all | solution.py:65
  68.4 19.0 %all-to-all-start.1 = ((bf16[8,16,1792]{2,1,0:T(8,128)(2,1)}), bf16[8,16,1792]{2,1,0:T(8,128)(2,1)S(1)}, u32[]{:S(2)}, u32[]{:S(2)}) async-start(bf16[8,16,1792]{2,1,0:T(8,128)(2,1)} %copy.82), calls=%async_computation.1 | async-start | bytes 917504 | tf_op jit(solution)/shard_map/all_to_all | solution.py:58
  73.5 43.0 %reduce-scatter.2.cloned.1.call-start = ((), (), s32[]{:S(2)}) async-start(), calls=%async_computation.8 | async-start | bytes 983040 | tf_op jit(solution)/shard_map/reduce_scatter | solution.py:79
  87.4 3.1 %copy-start.1 = (bf16[1,1792,1024]{2,1,0:T(8,128)(2,1)S(1)}, bf16[1,1792,1024]{2,1,0:T(8,128)(2,1)}, u32[]{:S(2)}) copy-start(bf16[1,1792,1024]{2,1,0:T(8,128)(2,1)} %param.11) | copy-start | bytes 11010052
  116.4 22.2 %copy-start.2 = (bf16[1,1792,1024]{2,1,0:T(8,128)(2,1)S(1)}, bf16[1,1792,1024]{2,1,0:T(8,128)(2,1)}, u32[]{:S(2)}) copy-start(bf16[1,1792,1024]{2,1,0:T(8,128)(2,1)} %param.10) | copy-start | bytes 11010052
  140.8 19.1 %all-to-all-start.5 = ((bf16[8,16,1792]{2,0,1:T(8,128)(2,1)}), bf16[8,16,1792]{2,0,1:T(8,128)(2,1)}, u32[]{:S(2)}, u32[]{:S(2)}) async-start(bf16[8,16,1792]{2,0,1:T(8,128)(2,1)} %copy.91), calls=%async_computation.6 | async-start | bytes 917504 | tf_op jit(solution)/shard_map/all_to_all | solution.py:128
  159.9 10.4 %all-to-all-start.3 = ((bf16[8,16,1792]{2,0,1:T(8,128)(2,1)}), bf16[8,16,1792]{2,0,1:T(8,128)(2,1)}, u32[]{:S(2)}, u32[]{:S(2)}) async-start(bf16[8,16,1792]{2,0,1:T(8,128)(2,1)} %copy.87), calls=%async_computation.4 | async-start | bytes 917504 | tf_op jit(solution)/shard_map/all_to_all | solution.py:121
  170.3 18.6 %all-to-all-start.6 = ((bf16[8,4,7168]{2,1,0:T(4,128)(2,1)}), bf16[8,4,7168]{2,1,0:T(4,128)(2,1)}, u32[]{:S(2)}, u32[]{:S(2)}) async-start(bf16[8,4,7168]{2,1,0:T(4,128)(2,1)} %all_to_all.65), calls=%async_computation.7 | async-start | bytes 917504 | tf_op jit(solution)/shard_map/all_to_all | solution.py:127
  189.0 18.1 %all-to-all-start.4 = ((bf16[8,4,7168]{2,1,0:T(4,128)(2,1)}), bf16[8,4,7168]{2,1,0:T(4,128)(2,1)}, u32[]{:S(2)}, u32[]{:S(2)}) async-start(bf16[8,4,7168]{2,1,0:T(4,128)(2,1)} %reshape.50), calls=%async_computation.5 | async-start | bytes 917504 | tf_op jit(solution)/shard_map/all_to_all | solution.py:120
Sparse Core Ops, SparseCore 0:
  92.3 24.1 reduce-scatter.1
